TPU v7x, 32 devices: a whole 2x2x4 slice. The times are simulated.
32 devices in a mesh: dp: 8 (over z, x), band: 4 (over y, core).
Axes of the slice: x: 2, y: 2, z: 4, core: 2. Of those that a mesh axis runs over, the one named last changes fastest.
Arguments:
- inputs: bfloat16 [2, 8, 2048, 768], P(None, 'dp', 'band'), may hold values from -6 to 6
- segments: int32 [2, 8, 2048], P(None, 'dp', 'band'), may hold values from 0 to 6, as said below
- cotangent: bfloat16 [2, 8, 2048, 768], P(None, 'dp', 'band'), may hold values from -6 to 6
- ln1_gain: bfloat16 [768], P('band'), may hold values from 0.5 to 1.5
- ln1_bias: bfloat16 [768], P('band'), may hold values from -3 to 3
- w_qkv: bfloat16 [768, 2304], P('band'), may hold values from -0.21875 to 0.21875
- b_qv: bfloat16 [1536], P('band'), may hold values from -0.4375 to 0.4375
- w_out: bfloat16 [768, 768], P('band'), may hold values from -2.5 to 2.5
- b_out: bfloat16 [768], P('band'), may hold values from -3 to 3
- ln2_gain: bfloat16 [768], P('band'), may hold values from 0.5 to 1.5
- ln2_bias: bfloat16 [768], P('band'), may hold values from -3 to 3
- w_up: bfloat16 [768, 3072], P('band'), may hold values from -0.21875 to 0.21875
- b_up: bfloat16 [3072], P('band'), may hold values from -3 to 3
- w_down: bfloat16 [3072, 768], P('band'), may hold values from -0.109375 to 0.109375
- b_down: bfloat16 [768], P('band'), may hold values from -3 to 3
Outputs:
- output: bfloat16 [2, 8, 2048, 768], P(None, 'dp', 'band')
- input_grad: bfloat16 [2, 8, 2048, 768], P(None, 'dp', 'band')
- grad_ln1_gain: float32 [768], P('band')
- grad_ln1_bias: float32 [768], P('band')
- grad_w_qkv: float32 [768, 2304], P('band')
- grad_b_qv: float32 [1536], P('band')
- grad_w_out: float32 [768, 768], P('band')
- grad_b_out: float32 [768], P('band')
- grad_ln2_gain: float32 [768], P('band')
- grad_ln2_bias: float32 [768], P('band')
- grad_w_up: float32 [768, 3072], P('band')
- grad_b_up: float32 [3072], P('band')
- grad_w_down: float32 [3072, 768], P('band')
- grad_b_down: float32 [768], P('band')
Inputs may be any that keep to these rules, and one draw needn't show every extreme that they name: `segments`: each sequence's 2048 slots are consecutive blocks of 512 slots that carry the same ids in the same order. In a block, ids never fall: tiles 1, 2, 3 and so on are contiguous runs, and padding (0) fills the end of the block, at most 51 slots.
All inputs are finite; a program needn't handle non-finite values.
Results may differ from a plain program's by a relative error of at most 0.02.
Values may be sent and summed in bfloat16 or wider, within the bound.
No kernel may reach another device: no remote copies, remote signals or barrier semaphores. Data moves between devices by JAX's collectives and lax.ppermute only.
A program may use at most 192 MiB of HBM per device.

v0:
```python
import jax
import jax.numpy as jnp
from jax import lax
from jax.sharding import PartitionSpec as P

HD = 64
D = 768


def inner_dot(left, right):
    return jnp.dot(left, right, preferred_element_type=jnp.float32)


def row_dot(left, right):
    return lax.dot_general(
        left, right, (((0,), (0,)), ((), ())), preferred_element_type=jnp.float32
    )


def col_dot(left, right):
    return lax.dot_general(
        left, right, (((1,), (1,)), ((), ())), preferred_element_type=jnp.float32
    )


def normed(value, gain, shift):
    center = value - jnp.mean(value, axis=-1, keepdims=True)
    spread = jnp.mean(center * center, axis=-1, keepdims=True)
    return center * lax.rsqrt(spread + 1e-06) * gain + shift


def gelu_tanh(value):
    return jax.nn.gelu(value, approximate=True)


def split_heads(block, heads):
    return block.reshape(block.shape[0], heads, -1).transpose(1, 0, 2)


def merge_heads(block):
    return block.transpose(1, 0, 2).reshape(block.shape[1], -1)


def blocks_of(array, count):
    return array.reshape((count, array.shape[0] // count) + array.shape[1:])


def masked_scores(query, keys, seg_query, seg_keys):
    scores = col_dot(query, keys) * 0.125
    return jnp.where(seg_query[:, None] == seg_keys[None, :], scores, -1e30)


def attend_forward(query, keys, values, seg_query, seg_keys, count):

    def per_head(item):
        head_query, head_keys, head_values = item

        def per_block(piece):
            block_query, block_seg = piece
            scores = masked_scores(block_query, head_keys, block_seg, seg_keys)
            peak = jnp.max(scores, axis=-1, keepdims=True)
            raised = jnp.exp(scores - peak)
            total = jnp.sum(raised, axis=-1, keepdims=True)
            weights = (raised / total).astype(jnp.bfloat16)
            return (inner_dot(weights, head_values), (peak + jnp.log(total))[:, 0])

        result, log_total = lax.map(
            per_block, (blocks_of(head_query, count), blocks_of(seg_query, count))
        )
        return (result.reshape(head_query.shape), log_total.reshape(-1))

    return lax.map(per_head, (query, keys, values))


def attend_backward(query, keys, values, grad_out, log_total, seg_query, seg_keys, count):

    def per_head(item):
        head_query, head_keys, head_values, head_grad, head_total = item

        def per_block(carry, piece):
            grad_keys, grad_values = carry
            block_query, block_grad, block_total, block_seg = piece
            scores = masked_scores(block_query, head_keys, block_seg, seg_keys)
            weights = jnp.exp(scores - block_total[:, None])
            grad_values = grad_values + row_dot(weights.astype(jnp.bfloat16), block_grad)
            grad_weights = col_dot(block_grad, head_values)
            center = jnp.sum(weights * grad_weights, axis=-1, keepdims=True)
            grad_scores = (weights * (grad_weights - center)).astype(jnp.bfloat16)
            grad_query = inner_dot(grad_scores, head_keys) * 0.125
            grad_keys = grad_keys + row_dot(grad_scores, block_query) * 0.125
            return ((grad_keys, grad_values), grad_query)

        start = jnp.zeros(head_keys.shape, jnp.float32)
        (grad_keys, grad_values), grad_query = lax.scan(
            per_block,
            (start, start),
            (
                blocks_of(head_query, count),
                blocks_of(head_grad, count),
                blocks_of(head_total, count),
                blocks_of(seg_query, count),
            ),
        )
        return (grad_query.reshape(head_query.shape), grad_keys, grad_values)

    return lax.map(per_head, (query, keys, values, grad_out, log_total))


def layer_pass(inputs, segment, cotangent, whole, parts):
    (
        gain_one,
        shift_one,
        w_proj,
        b_proj,
        w_mix,
        b_mix,
        gain_two,
        shift_two,
        w_rise,
        b_rise,
        w_fall,
        b_fall,
    ) = whole
    gain_one = gain_one.astype(jnp.float32)
    shift_one = shift_one.astype(jnp.float32)
    gain_two = gain_two.astype(jnp.float32)
    shift_two = shift_two.astype(jnp.float32)
    b_proj = b_proj.astype(jnp.float32)
    b_mix = b_mix.astype(jnp.float32)
    b_rise = b_rise.astype(jnp.float32)
    b_fall = b_fall.astype(jnp.float32)
    heads = D // HD
    count = max(inputs.shape[0] // 512, 1)
    value = inputs.astype(jnp.float32)
    normed_in, pull_one = jax.vjp(normed, value, gain_one, shift_one)
    normed_low = normed_in.astype(jnp.bfloat16)
    projected = inner_dot(normed_low, w_proj)
    query = (projected[:, :D] + b_proj[:D]).astype(jnp.bfloat16)
    key_part = projected[:, D : 2 * D].astype(jnp.bfloat16)
    value_part = (projected[:, 2 * D :] + b_proj[D:]).astype(jnp.bfloat16)
    keys_all, values_all = (
        lax.all_gather(key_part, "band", axis=0, tiled=True),
        lax.all_gather(value_part, "band", axis=0, tiled=True),
    )
    seg_keys = jnp.tile(segment, parts)
    query_heads = split_heads(query, heads)
    keys_heads = split_heads(keys_all, heads)
    values_heads = split_heads(values_all, heads)
    head_out, log_total = attend_forward(
        query_heads, keys_heads, values_heads, segment, seg_keys, count
    )
    mixed = merge_heads(head_out).astype(jnp.bfloat16)
    hidden = value + (inner_dot(mixed, w_mix) + b_mix)
    normed_mid, pull_two = jax.vjp(normed, hidden, gain_two, shift_two)
    mid_low = normed_mid.astype(jnp.bfloat16)
    upward = inner_dot(mid_low, w_rise) + b_rise
    active, pull_gelu = jax.vjp(gelu_tanh, upward)
    active_low = active.astype(jnp.bfloat16)
    output = hidden + (inner_dot(active_low, w_fall) + b_fall)
    grad_y = cotangent.astype(jnp.float32) * (segment != 0).astype(jnp.float32)[:, None]
    grad_m = grad_y.astype(jnp.bfloat16)
    grad_w_fall = row_dot(active_low, grad_m)
    grad_b_fall = jnp.sum(grad_m.astype(jnp.float32), axis=0)
    grad_up = pull_gelu(col_dot(grad_m, w_fall))[0].astype(jnp.bfloat16)
    grad_w_rise = row_dot(mid_low, grad_up)
    grad_b_rise = jnp.sum(grad_up.astype(jnp.float32), axis=0)
    grad_mid, grad_gain_two, grad_shift_two = pull_two(col_dot(grad_up, w_rise))
    grad_hidden = grad_y + grad_mid
    grad_a = grad_hidden.astype(jnp.bfloat16)
    grad_w_mix = row_dot(mixed, grad_a)
    grad_b_mix = jnp.sum(grad_a.astype(jnp.float32), axis=0)
    grad_mixed = col_dot(grad_a, w_mix).astype(jnp.bfloat16)
    grad_heads = split_heads(grad_mixed, heads)
    grad_query, grad_keys, grad_values = attend_backward(
        query_heads, keys_heads, values_heads, grad_heads, log_total, segment, seg_keys, count
    )
    keys_sum, values_sum = (
        lax.psum_scatter(
            merge_heads(grad_keys).astype(jnp.bfloat16), "band", scatter_dimension=0, tiled=True
        ).astype(jnp.float32),
        lax.psum_scatter(
            merge_heads(grad_values).astype(jnp.bfloat16), "band", scatter_dimension=0, tiled=True
        ).astype(jnp.float32),
    )
    query_low = merge_heads(grad_query).astype(jnp.bfloat16)
    values_low = values_sum.astype(jnp.bfloat16)
    grad_qkv = jnp.concatenate([query_low, keys_sum.astype(jnp.bfloat16), values_low], axis=1)
    grad_w_proj = row_dot(normed_low, grad_qkv)
    grad_b_proj = jnp.concatenate(
        [
            jnp.sum(query_low.astype(jnp.float32), axis=0),
            jnp.sum(values_low.astype(jnp.float32), axis=0),
        ]
    )
    grad_norm_in, grad_gain_one, grad_shift_one = pull_one(col_dot(grad_qkv, w_proj))
    grad_input = grad_hidden + grad_norm_in
    grads = (
        grad_gain_one,
        grad_shift_one,
        grad_w_proj,
        grad_b_proj,
        grad_w_mix,
        grad_b_mix,
        grad_gain_two,
        grad_shift_two,
        grad_w_rise,
        grad_b_rise,
        grad_w_fall,
        grad_b_fall,
    )
    return (output.astype(jnp.bfloat16), grad_input.astype(jnp.bfloat16), grads)


def gather_each(shards):
    return (
        lax.all_gather(shards[0], "band", axis=0, tiled=True),
        lax.all_gather(shards[1], "band", axis=0, tiled=True),
        lax.all_gather(shards[2], "band", axis=0, tiled=True),
        lax.all_gather(shards[3], "band", axis=0, tiled=True),
        lax.all_gather(shards[4], "band", axis=0, tiled=True),
        lax.all_gather(shards[5], "band", axis=0, tiled=True),
        lax.all_gather(shards[6], "band", axis=0, tiled=True),
        lax.all_gather(shards[7], "band", axis=0, tiled=True),
        lax.all_gather(shards[8], "band", axis=0, tiled=True),
        lax.all_gather(shards[9], "band", axis=0, tiled=True),
        lax.all_gather(shards[10], "band", axis=0, tiled=True),
        lax.all_gather(shards[11], "band", axis=0, tiled=True),
    )


def reduce_end(grads):
    shares = (
        lax.psum_scatter(
            grads[0].astype(jnp.bfloat16), "band", scatter_dimension=0, tiled=True
        ).astype(jnp.float32),
        lax.psum_scatter(
            grads[1].astype(jnp.bfloat16), "band", scatter_dimension=0, tiled=True
        ).astype(jnp.float32),
        lax.psum_scatter(
            grads[2].astype(jnp.bfloat16), "band", scatter_dimension=0, tiled=True
        ).astype(jnp.float32),
        lax.psum_scatter(
            grads[3].astype(jnp.bfloat16), "band", scatter_dimension=0, tiled=True
        ).astype(jnp.float32),
        lax.psum_scatter(
            grads[4].astype(jnp.bfloat16), "band", scatter_dimension=0, tiled=True
        ).astype(jnp.float32),
        lax.psum_scatter(
            grads[5].astype(jnp.bfloat16), "band", scatter_dimension=0, tiled=True
        ).astype(jnp.float32),
        lax.psum_scatter(
            grads[6].astype(jnp.bfloat16), "band", scatter_dimension=0, tiled=True
        ).astype(jnp.float32),
        lax.psum_scatter(
            grads[7].astype(jnp.bfloat16), "band", scatter_dimension=0, tiled=True
        ).astype(jnp.float32),
        lax.psum_scatter(
            grads[8].astype(jnp.bfloat16), "band", scatter_dimension=0, tiled=True
        ).astype(jnp.float32),
        lax.psum_scatter(
            grads[9].astype(jnp.bfloat16), "band", scatter_dimension=0, tiled=True
        ).astype(jnp.float32),
        lax.psum_scatter(
            grads[10].astype(jnp.bfloat16), "band", scatter_dimension=0, tiled=True
        ).astype(jnp.float32),
        lax.psum_scatter(
            grads[11].astype(jnp.bfloat16), "band", scatter_dimension=0, tiled=True
        ).astype(jnp.float32),
    )
    return (
        lax.psum(shares[0].astype(jnp.bfloat16), "dp").astype(jnp.float32),
        lax.psum(shares[1].astype(jnp.bfloat16), "dp").astype(jnp.float32),
        lax.psum(shares[2].astype(jnp.bfloat16), "dp").astype(jnp.float32),
        lax.psum(shares[3].astype(jnp.bfloat16), "dp").astype(jnp.float32),
        lax.psum(shares[4].astype(jnp.bfloat16), "dp").astype(jnp.float32),
        lax.psum(shares[5].astype(jnp.bfloat16), "dp").astype(jnp.float32),
        lax.psum(shares[6].astype(jnp.bfloat16), "dp").astype(jnp.float32),
        lax.psum(shares[7].astype(jnp.bfloat16), "dp").astype(jnp.float32),
        lax.psum(shares[8].astype(jnp.bfloat16), "dp").astype(jnp.float32),
        lax.psum(shares[9].astype(jnp.bfloat16), "dp").astype(jnp.float32),
        lax.psum(shares[10].astype(jnp.bfloat16), "dp").astype(jnp.float32),
        lax.psum(shares[11].astype(jnp.bfloat16), "dp").astype(jnp.float32),
    )


def body(
    inputs,
    segments,
    cotangent,
    ln1_gain,
    ln1_bias,
    w_qkv,
    b_qv,
    w_out,
    b_out,
    ln2_gain,
    ln2_bias,
    w_up,
    b_up,
    w_down,
    b_down,
):
    shards = (
        ln1_gain,
        ln1_bias,
        w_qkv,
        b_qv,
        w_out,
        b_out,
        ln2_gain,
        ln2_bias,
        w_up,
        b_up,
        w_down,
        b_down,
    )
    parts = lax.axis_size("band")
    results = []
    grads_in = []
    totals = None
    for batch in range(inputs.shape[0]):
        whole = gather_each(shards)
        result, grad_in, grads = layer_pass(
            inputs[batch, 0], segments[batch, 0], cotangent[batch, 0], whole, parts
        )
        totals = (
            grads
            if totals is None
            else tuple((first + second for first, second in zip(totals, grads)))
        )
        results.append(result)
        grads_in.append(grad_in)
    totals = reduce_end(totals)
    return (jnp.stack(results)[:, None], jnp.stack(grads_in)[:, None]) + tuple(totals)


def solution(mesh):
    return jax.shard_map(
        body,
        mesh=mesh,
        in_specs=(
            P(None, "dp", "band", None),
            P(None, "dp", "band"),
            P(None, "dp", "band", None),
            P("band"),
            P("band"),
            P("band", None),
            P("band"),
            P("band", None),
            P("band"),
            P("band"),
            P("band"),
            P("band", None),
            P("band"),
            P("band", None),
            P("band"),
        ),
        out_specs=(
            P(None, "dp", "band", None),
            P(None, "dp", "band", None),
            P("band"),
            P("band"),
            P("band", None),
            P("band"),
            P("band", None),
            P("band"),
            P("band"),
            P("band"),
            P("band", None),
            P("band"),
            P("band", None),
            P("band"),
        ),
        check_vma=False,
    )
```

profile of v0, /device:TPU:0, one launch (start us, length us, event | category | flops | bytes accessed | tf_op | source)
XLA Modules:
  0.0 1097.1 jit_solution(7388853677042379467)
XLA Ops:
  14.2 13.5 %all-reduce.17 = (bf16[768]{0:T(1024)(128)(2,1)S(1)}, bf16[768]{0:T(1024)(128)(2,1)S(1)}, bf16[768]{0:T(1024)(128)(2,1)S(1)}, bf16[768]{0:T(1024)(128)(2,1)S(1)}, bf16[768]{0:T(1024)(128)(2,1)S(1)}) all-reduce(bf16[768]{0:T(1024)(128)(2,1)S(1)} %dynamic-update-slice.1, ...), channel_id=1, replica_groups=mesh['dp'=8,'band'=4] {'band'}, use_global_device_ids=true, to_apply=%add.1 | all-reduce | flops 3840 | bytes 15360
  28.3 5.3 all-gather
  36.6 6.6 all-gather.11.cloned.1.call-done
  43.2 4.3 fusion.162
  60.4 5.3 all-gather.1
  73.9 7.5 all-gather.25.cloned.1.call-done
  81.5 4.8 copy.71
  86.2 6.7 copy.74
  93.0 19.2 %all-gather.23.cloned.1.call-done = bf16[2048,768]{1,0:T(8,128)(2,1)} async-done(((bf16[512,768]{1,0:T(8,128)(2,1)}), bf16[2048,768]{1,0:T(8,128)(2,1)}) %all-gather.23.cloned.1.call-update) | async-done | bytes 3145744 | tf_op jit(solution)/shard_map/all_gather | solution.py:142
  112.2 4.7 copy.70
  116.9 6.7 copy.73
  124.6 104.7 %while.51 = (s32[]{:T(128)}, bf16[12,512,64]{1,2,0:T(8,128)(2,1)}, f32[12,512]{1,0:T(8,128)S(1)}, s32[1,1,512]{2,1,0:T(1,128)S(1)}, bf16[12,512,64]{2,1,0:T(8,12...) while((s32[]{:T(128)}, bf16[12,512,64]{1,2,0:T(8,128)(2,1)}, ...), condition=%wide.region_13.14_spmd.clone, body=%wide.region_10.13_spmd.clone.sunk | while | flops 277872128 | bytes 30730372 | solution.py:72
  129.3 3.9 fusion.255
  138.0 3.9 fusion.255
  146.7 3.9 fusion.255
  155.4 3.9 fusion.255
  164.0 3.9 fusion.255
  172.7 3.9 fusion.255
  181.3 3.9 fusion.255
  190.0 3.9 fusion.255
  198.7 4.4 fusion.255
  207.9 3.9 fusion.255
  216.6 4.0 fusion.255
  225.3 4.0 fusion.255
  229.3 5.3 copy.65
  234.6 6.7 copy.68
  241.3 4.8 copy.64
  246.1 6.6 copy.67
  252.7 97.4 %while.50 = (s32[]{:T(128)}, bf16[12,512,64]{1,2,0:T(8,128)(2,1)S(1)}, f32[12,512]{1,0:T(8,128)S(1)}, s32[1,1,512]{2,1,0:T(1,128)S(1)}, bf16[12,512,64]{2,1,0:T(...) while((s32[]{:T(128)}, ...), condition=%wide.region_5.6_spmd.clone, body=%wide.region_2.5_spmd.clone.sunk | while | flops 277872128 | bytes 30730372 | solution.py:72
  257.6 3.3 fusion.251
  265.7 3.3 fusion.251
  273.8 3.3 fusion.251
  281.9 3.3 fusion.251
  290.0 3.3 fusion.251
  298.2 3.3 fusion.251
  314.4 3.3 fusion.251
  330.6 3.3 fusion.251
  346.8 3.3 fusion.251
  356.3 7.3 fusion.171
  363.6 5.0 fusion.170
  368.6 9.7 convert_reduce_fusion.1
  378.4 6.2 fusion.182
  385.1 8.8 convert_reduce_fusion
  394.0 3.8 multiply_reduce_fusion.2
  407.9 130.6 %while.52 = (s32[]{:T(128)}, bf16[12,512,64]{1,2,0:T(8,128)(2,1)}, bf16[12,2048,64]{1,2,0:T(8,128)(2,1)S(1)}, bf16[12,2048,64]{1,2,0:T(8,128)(2,1)}, s32[1,1,512...) while((s32[]{:T(128)}, bf16[12,512,64]{1,2,0:T(8,128)(2,1)}, ...), condition=%wide.region_20.21_spmd.clone, body=%wide.region_18.20_spmd.clone.sunk | while | flops 681737728 | bytes 34655352 | solution.py:106
  538.5 4.3 convolution_convert_fusion
  548.6 139.4 %while.53 = (s32[]{:T(128)}, bf16[12,512,64]{1,2,0:T(8,128)(2,1)}, bf16[12,2048,64]{1,2,0:T(8,128)(2,1)S(1)}, bf16[12,2048,64]{1,2,0:T(8,128)(2,1)}, s32[1,1,512...) while((s32[]{:T(128)}, bf16[12,512,64]{1,2,0:T(8,128)(2,1)}, ...), condition=%wide.region_29.30_spmd.clone, body=%wide.region_27.29_spmd.clone.sunk | while | flops 681737728 | bytes 34655352 | solution.py:106
  693.8 6.4 fusion.150
  700.2 9.0 add_convert_fusion
  709.9 5.4 fusion.169
  715.3 4.9 add_convert_fusion.1
  721.6 6.9 fusion.135
  728.5 39.2 %reduce-scatter.15.cloned.1.call-done = bf16[512,768]{0,1:T(8,128)(2,1)} async-done(((bf16[2048,768]{0,1:T(8,128)(2,1)}), bf16[512,768]{0,1:T(8,128)(2,1)}) %reduce-scatter.15.cloned.1.call-update) | async-done | bytes 786448 | tf_op jit(solution)/shard_map/reduce_scatter | solution.py:181
  767.7 7.9 add_convert_fusion.2
  782.2 4.9 fusion.134
  787.2 4.4 fusion.121
  796.5 50.4 %reduce-scatter.23.cloned.1.call-done = bf16[768,768]{1,0:T(8,128)(2,1)} async-done(((bf16[3072,768]{1,0:T(8,128)(2,1)}), bf16[768,768]{1,0:T(8,128)(2,1)}) %reduce-scatter.23.cloned.1.call-update) | async-done | bytes 1179664 | tf_op jit(solution)/shard_map/reduce_scatter | solution.py:263
  846.9 50.4 %reduce-scatter.21.cloned.1.call-done = bf16[192,3072]{1,0:T(8,128)(2,1)} async-done(((bf16[768,3072]{1,0:T(8,128)(2,1)}), bf16[192,3072]{1,0:T(8,128)(2,1)}) %reduce-scatter.21.cloned.1.call-update) | async-done | bytes 1179664 | tf_op jit(solution)/shard_map/reduce_scatter | solution.py:257
  897.3 42.8 %reduce-scatter.17.cloned.1.call-done = bf16[192,2304]{1,0:T(8,128)(2,1)} async-done(((bf16[768,2304]{1,0:T(8,128)(2,1)}), bf16[192,2304]{1,0:T(8,128)(2,1)}) %reduce-scatter.17.cloned.1.call-update) | async-done | bytes 884752 | tf_op jit(solution)/shard_map/reduce_scatter | solution.py:239
  941.5 10.5 all-reduce.16
  952.6 23.1 %all-reduce.14 = (bf16[192]{0:T(256)(128)(2,1)S(1)}, bf16[192]{0:T(256)(128)(2,1)S(1)}, bf16[384]{0:T(512)(128)(2,1)S(1)}, bf16[192]{0:T(256)(128)(2,1)S(1)}, bf...) all-reduce(bf16[192]{0:T(256)(128)(2,1)S(1)} %dynamic-slice.7, ...), channel_id=1, replica_groups=mesh['dp'=8,'band'=4] {'dp'}, use_global_device_ids=true, to_apply=%region_37.38 | all-reduce | flops 2304 | bytes 9216 | tf_op jit(solution)/shard_map/psum | solution.py:271
  984.6 8.3 fusion.132
  992.9 8.3 fusion.133
  1002.5 81.1 %all-reduce.20.cloned.1.call-done = (bf16[192,2304]{1,0:T(8,128)(2,1)}, bf16[192,768]{1,0:T(8,128)(2,1)}, bf16[192,3072]{1,0:T(8,128)(2,1)}, bf16[768,768]{1,0:T(8,128)(2,1)}) async-done(((bf16[192,2304]{1,0:T(8,128)(2,1)}, bf16[192,768]{1,0:T(8,128)(2,1)}, bf16[192,3072]{1,0:T(8,128)(2,1)}, bf16[768,768]{1,0:T(8,128)(2,1)}), (bf16[192,2304]{1,0:T(8,128)(2,1)}, bf16[192,768]{1,0:T(8,128)(2,1)}, ...) | async-done | bytes 3538960 | tf_op jit(solution)/shard_map/psum | solution.py:273
  (733 shorter events, 483.6 us)
Async XLA Ops:
  7.2 28.2 %copy-start.2 = (bf16[2,1,512,768]{3,2,1,0:T(8,128)(2,1)S(1)}, bf16[2,1,512,768]{3,2,1,0:T(8,128)(2,1)}, u32[]{:S(2)}) copy-start(bf16[2,1,512,768]{3,2,1,0:T(8,128)(2,1)} %param.23) | copy-start | bytes 4718596
  7.2 36.0 %all-gather.11.cloned.1.call-start = ((), (), s32[]{:S(2)}) async-start(), calls=%async_computation.8 | async-start | bytes 4423680 | tf_op jit(solution)/shard_map/all_gather | solution.py:218
  7.9 73.6 %all-gather.25.cloned.1.call-start = ((), (), s32[]{:S(2)}) async-start(), calls=%async_computation.15 | async-start | bytes 3932160 | tf_op jit(solution)/shard_map/all_gather | solution.py:143
  27.6 19.9 %copy-start.37 = (f32[768]{0:T(1024)}, f32[768]{0:T(1024)S(1)}, u32[]{:S(2)}) copy-start(f32[768]{0:T(1024)S(1)} %convert_element_type.378) | copy-start | bytes 9220
  27.7 19.9 %copy-start.60 = (f32[768]{0:T(1024)}, f32[768]{0:T(1024)S(1)}, u32[]{:S(2)}) copy-start(f32[768]{0:T(1024)S(1)} %convert_element_type.379) | copy-start | bytes 9220
  35.4 12.2 %copy-start.40 = (f32[512]{0:T(512)}, f32[512]{0:T(512)S(1)}, u32[]{:S(2)}) copy-start(f32[512]{0:T(512)S(1)} %get-tuple-element.718) | copy-start | bytes 6148
  35.4 12.2 %copy-start.42 = (f32[512]{0:T(512)}, f32[512]{0:T(512)S(1)}, u32[]{:S(2)}) copy-start(f32[512]{0:T(512)S(1)} %get-tuple-element.719) | copy-start | bytes 6148
  36.6 11.0 copy-start.46
  36.6 11.0 copy-start.44
  43.2 4.4 copy-start.72
  52.7 59.5 %all-gather.23.cloned.1.call-start = ((), (), s32[]{:S(2)}) async-start(), calls=%async_computation.14 | async-start | bytes 3932160 | tf_op jit(solution)/shard_map/all_gather | solution.py:142
  55.1 174.1 %all-gather.15.cloned.1.call-start = ((), (), s32[]{:S(2)}) async-start(), calls=%async_computation.10 | async-start | bytes 3932160 | tf_op jit(solution)/shard_map/all_gather | solution.py:143
  55.7 4.6 copy-start.64
  55.7 4.7 copy-start.69
  55.8 185.5 %all-gather.13.cloned.1.call-start = ((), (), s32[]{:S(2)}) async-start(), calls=%async_computation.9 | async-start | bytes 3932160 | tf_op jit(solution)/shard_map/all_gather | solution.py:142
  58.2 291.9 %all-gather.17.cloned.1.call-start = ((), (), s32[]{:S(2)}) async-start(), calls=%async_computation.11 | async-start | bytes 1474560 | tf_op jit(solution)/shard_map/all_gather | solution.py:220
  58.8 297.5 %all-gather.19.cloned.1.call-start = ((), (), s32[]{:S(2)}) async-start(), calls=%async_computation.12 | async-start | bytes 5898240 | tf_op jit(solution)/shard_map/all_gather | solution.py:224
  59.5 309.1 %all-gather.21.cloned.1.call-start = ((), (), s32[]{:S(2)}) async-start(), calls=%async_computation.13 | async-start | bytes 5898240 | tf_op jit(solution)/shard_map/all_gather | solution.py:226
  60.3 660.2 %reduce-scatter.11.cloned.1.call-start = ((), (), s32[]{:S(2)}) async-start(), calls=%async_computation.17 | async-start | bytes 3932160 | tf_op jit(solution)/shard_map/reduce_scatter | solution.py:181
  60.4 303.2 %copy-start.62 = (f32[768]{0:T(1024)}, f32[768]{0:T(1024)S(1)}, u32[]{:S(2)}) copy-start(f32[768]{0:T(1024)S(1)} %convert_element_type.389) | copy-start | bytes 9220
  229.2 5.3 copy-start.20
  229.2 5.3 copy-start.34
  229.2 5.3 copy-start.39
  353.6 44.2 %copy-start.13 = (f32[512,768]{1,0:T(8,128)}, f32[512,768]{1,0:T(8,128)S(1)}, u32[]{:S(2)}) copy-start(f32[512,768]{1,0:T(8,128)S(1)} %get-tuple-element.709) | copy-start | bytes 4718596
  356.3 7.3 copy-start.17
  356.3 7.3 copy-start.71
  363.6 5.0 copy-start.10
  378.4 6.2 copy-start.79
  378.4 6.2 copy-start.70
  378.4 6.8 copy-start.78
  378.4 15.6 %slice-start = ((s8[4718592]{0:T(1024)(128)(4,1)}), s8[4194304]{0:T(1024)(128)(4,1)S(1)}, s32[]{:S(2)}) async-start(s8[4718592]{0:T(1024)(128)(4,1)} %bitcast.463), calls=%async_computation.25 | async-start | bytes 8388608
  385.1 8.8 copy-start.18
  385.1 8.8 slice-start.1
  393.9 3.8 copy-start.80
  538.5 4.4 copy-start.9
  538.5 182.0 %reduce-scatter.9.cloned.1.call-start = ((), (), s32[]{:S(2)}) async-start(), calls=%async_computation.16 | async-start | bytes 3932160 | tf_op jit(solution)/shard_map/reduce_scatter | solution.py:178
  545.1 183.3 %reduce-scatter.13.cloned.1.call-start = ((), (), s32[]{:S(2)}) async-start(), calls=%async_computation.18 | async-start | bytes 3932160 | tf_op jit(solution)/shard_map/reduce_scatter | solution.py:178
  689.7 78.0 %reduce-scatter.15.cloned.1.call-start = ((), (), s32[]{:S(2)}) async-start(), calls=%async_computation.19 | async-start | bytes 3932160 | tf_op jit(solution)/shard_map/reduce_scatter | solution.py:181
  690.3 106.2 %reduce-scatter.19.cloned.1.call-start = ((), (), s32[]{:S(2)}) async-start(), calls=%async_computation.21 | async-start | bytes 1474560 | tf_op jit(solution)/shard_map/reduce_scatter | solution.py:245
  693.7 153.2 %reduce-scatter.23.cloned.1.call-start = ((), (), s32[]{:S(2)}) async-start(), calls=%async_computation.23 | async-start | bytes 5898240 | tf_op jit(solution)/shard_map/reduce_scatter | solution.py:263
  709.2 6.0 copy-start.14
  709.2 188.0 %reduce-scatter.21.cloned.1.call-start = ((), (), s32[]{:S(2)}) async-start(), calls=%async_computation.22 | async-start | bytes 5898240 | tf_op jit(solution)/shard_map/reduce_scatter | solution.py:257
  709.9 5.4 copy-start.81
  720.2 219.9 %reduce-scatter.17.cloned.1.call-start = ((), (), s32[]{:S(2)}) async-start(), calls=%async_computation.20 | async-start | bytes 4423680 | tf_op jit(solution)/shard_map/reduce_scatter | solution.py:239
  721.6 46.1 %copy-start.41 = (f32[512]{0:T(512)S(1)}, f32[512]{0:T(512)}, u32[]{:S(2)}) copy-start(f32[512]{0:T(512)} %copy-done.40) | copy-start | bytes 6148
  721.6 46.1 %copy-start.45 = (f32[512]{0:T(512)S(1)}, f32[512]{0:T(512)}, u32[]{:S(2)}) copy-start(f32[512]{0:T(512)} %copy-done.44) | copy-start | bytes 6148
  775.6 5.2 copy-start.67
  775.6 5.2 copy-start.68
  775.6 5.2 copy-start.65
  775.6 5.2 copy-start.66
  775.6 5.2 copy-start.56
  775.6 5.2 copy-start.57
  775.6 5.2 copy-start.58
  775.6 5.2 copy-start.59
  775.6 307.9 %all-reduce.20.cloned.1.call-start = ((), (), s32[]{:S(2)}) async-start(), calls=%async_computation.24 | async-start | bytes 7077888 | tf_op jit(solution)/shard_map/psum | solution.py:273
  782.2 4.9 copy-start.33
  782.2 4.9 copy-start.73
  782.2 4.9 copy-start.76
  787.1 4.5 copy-start.12
  787.2 4.4 copy-start.55
  787.2 4.4 copy-start.53
  795.3 185.0 %copy-start.5 = (f32[512,768]{1,0:T(8,128)S(1)}, f32[512,768]{1,0:T(8,128)}, u32[]{:S(2)}) copy-start(f32[512,768]{1,0:T(8,128)} %copy-done.4) | copy-start | bytes 4718596
  795.3 185.0 %copy-start.49 = (f32[512]{0:T(512)S(1)}, f32[512]{0:T(512)}, u32[]{:S(2)}) copy-start(f32[512]{0:T(512)} %copy-done.48) | copy-start | bytes 6148
  984.6 8.3 copy-start.15
  (59 other events, 113.2 us)
Sparse Core Ops, SparseCore 0:
  9.6 33.6 all-gather.10
  52.8 28.6 all-gather.24
  83.6 28.4 all-gather.22
  114.2 28.5 all-gather.14
  144.1 28.5 all-gather.12
  174.1 17.4 all-gather.16
  193.1 37.4 all-gather.18
  232.1 37.4 all-gather.20
  538.6 37.8 reduce-scatter.10
  578.8 37.7 reduce-scatter.8
  689.8 37.6 reduce-scatter.12
  729.9 37.7 reduce-scatter.14
  770.8 25.6 reduce-scatter.18
  798.9 47.9 reduce-scatter.22
  849.3 47.9 reduce-scatter.20
  899.7 40.3 reduce-scatter.16
  943.9 139.5 all-reduce.19
where the time goes:
time: 1110 us; the launch traced here: 1100 us
  matrix products  508 us (46%)
  waiting for transfers between devices  302 us (27%)
  local copies, waits for them, and re-layouts  147 us (13%)
  other arithmetic  61.3 us (6%)
  blocking collectives  57.8 us (5%)
  between operations  18 us (2%)
    dot_general x80, matrix products, col_dot(): lax.dot_general(left, right, (((1,), (1,)), ((), ())), preferred_element_...  197 us
    dot_general x56, matrix products, inner_dot(): return jnp.dot(left, right, preferred_element_type=jnp.float32)  184 us
    dot_general x56, matrix products, row_dot(): lax.dot_general(left, right, (((0,), (0,)), ((), ())), preferred_element_...  127 us
    psum x1, waiting for transfers between devices, reduce_end(): lax.psum(shares[2].astype(jnp.bfloat16), 'dp').astype(jnp.float32)  81.1 us
    reduce_scatter x1, waiting for transfers between devices, reduce_end(): lax.psum_scatter(grads[10].astype(jnp.bfloat16), 'band', scatter_dimensio...  50.4 us
    reduce_scatter x1, waiting for transfers between devices, reduce_end(): lax.psum_scatter(grads[8].astype(jnp.bfloat16), 'band', scatter_dimension...  50.4 us
    while x144, local copies, waits for them, and re-layouts  49.5 us
    unnamed x193, local copies, waits for them, and re-layouts  47.8 us
  transfers between devices with their start and end apart: 17, of which 9 were waited for; matrix products, arithmetic and copies ran while one was open for 43% of the time, Pallas kernels for 0%

commit v1 on v0

--- a/solution.py
+++ b/solution.py
@@ -268,7 +268,9 @@
         ).astype(jnp.float32),
     )
     return (
-        lax.psum(shares[0].astype(jnp.bfloat16), "dp").astype(jnp.float32),
+        jnp.sum(jax.lax.all_gather(shares[0].astype(jnp.bfloat16), axis_name="dp"), axis=0).astype(
+            jnp.float32
+        ),
         lax.psum(shares[1].astype(jnp.bfloat16), "dp").astype(jnp.float32),
         lax.psum(shares[2].astype(jnp.bfloat16), "dp").astype(jnp.float32),
         lax.psum(shares[3].astype(jnp.bfloat16), "dp").astype(jnp.float32),

time: 1110 us -> 1110 us (level)
    unnamed x2 -> x3, blocking collectives: 24 us -> 47.8 us
    psum x1 -> x0, blocking collectives: 23.1 us -> none  [reduce_end(): lax.psum(shares[0].astype(jnp.bfloat16), 'dp').astype(jnp.float32)]
    unnamed x193 -> x198, local copies, waits for them, and re-layouts: 47.8 us -> 49 us
  transfers between devices with their start and end apart: 17 -> 17, of which waited for: 9 -> 8; matrix products, arithmetic and copies ran while one was open for 43% -> 43% of each run, Pallas kernels for 0% -> 0%
where the time goes in v1:
time: 1110 us; the launch traced here: 1100 us
  matrix products  508 us (46%)
  waiting for transfers between devices  300 us (27%)
  local copies, waits for them, and re-layouts  148 us (13%)
  other arithmetic  61.3 us (6%)
  blocking collectives  58.4 us (5%)
  between operations  18.7 us (2%)
    dot_general x80, matrix products, col_dot(): lax.dot_general(left, right, (((1,), (1,)), ((), ())), preferred_element_...  197 us
    dot_general x56, matrix products, inner_dot(): return jnp.dot(left, right, preferred_element_type=jnp.float32)  184 us
    dot_general x56, matrix products, row_dot(): lax.dot_general(left, right, (((0,), (0,)), ((), ())), preferred_element_...  126 us
    psum x1, waiting for transfers between devices, reduce_end(): lax.psum(shares[2].astype(jnp.bfloat16), 'dp').astype(jnp.float32)  80.3 us
    reduce_scatter x1, waiting for transfers between devices, reduce_end(): lax.psum_scatter(grads[8].astype(jnp.bfloat16), 'band', scatter_dimension...  50.4 us
    reduce_scatter x1, waiting for transfers between devices, reduce_end(): lax.psum_scatter(grads[10].astype(jnp.bfloat16), 'band', scatter_dimensio...  49.8 us
    while x144, local copies, waits for them, and re-layouts  49.3 us
    unnamed x198, local copies, waits for them, and re-layouts  49 us
  transfers between devices with their start and end apart: 17, of which 8 were waited for; matrix products, arithmetic and copies ran while one was open for 43% of the time, Pallas kernels for 0%

profile of v1, /device:TPU:0, one launch (start us, length us, event | category | flops | bytes accessed | tf_op | source)
XLA Modules:
  0.0 1097.1 jit_solution(10220737343310803131)
XLA Ops:
  14.2 13.5 %all-reduce.18 = (bf16[768]{0:T(1024)(128)(2,1)S(1)}, bf16[768]{0:T(1024)(128)(2,1)S(1)}, bf16[768]{0:T(1024)(128)(2,1)S(1)}, bf16[768]{0:T(1024)(128)(2,1)S(1)}, bf16[768]{0:T(1024)(128)(2,1)S(1)}) all-reduce(bf16[768]{0:T(1024)(128)(2,1)S(1)} %dynamic-update-slice.1, ...), channel_id=1, replica_groups=mesh['dp'=8,'band'=4] {'band'}, use_global_device_ids=true, to_apply=%add.1 | all-reduce | flops 3840 | bytes 15360
  28.3 5.3 all-gather.1
  36.6 6.6 all-gather.12.cloned.1.call-done
  43.2 4.3 fusion.162
  60.5 5.3 all-gather.2
  74.0 7.5 all-gather.26.cloned.1.call-done
  81.5 4.8 copy.95
  86.3 6.7 copy.98
  93.0 19.2 %all-gather.24.cloned.1.call-done = bf16[2048,768]{1,0:T(8,128)(2,1)} async-done(((bf16[512,768]{1,0:T(8,128)(2,1)}), bf16[2048,768]{1,0:T(8,128)(2,1)}) %all-gather.24.cloned.1.call-update) | async-done | bytes 3145744 | tf_op jit(solution)/shard_map/all_gather | solution.py:142
  112.2 4.7 copy.94
  116.9 6.7 copy.97
  124.6 104.6 %while.51 = (s32[]{:T(128)}, bf16[12,512,64]{1,2,0:T(8,128)(2,1)}, f32[12,512]{1,0:T(8,128)S(1)}, s32[1,1,512]{2,1,0:T(1,128)S(1)}, bf16[12,512,64]{2,1,0:T(8,12...) while((s32[]{:T(128)}, bf16[12,512,64]{1,2,0:T(8,128)(2,1)}, ...), condition=%wide.region_13.14_spmd.clone, body=%wide.region_10.13_spmd.clone.sunk | while | flops 277872128 | bytes 30730372 | solution.py:72
  129.3 3.9 fusion.255
  138.0 3.9 fusion.255
  146.6 3.9 fusion.255
  155.3 3.9 fusion.255
  164.0 3.9 fusion.255
  172.6 3.9 fusion.255
  181.3 3.9 fusion.255
  190.0 3.9 fusion.255
  198.7 4.4 fusion.255
  207.8 3.9 fusion.255
  216.5 3.9 fusion.255
  225.2 3.9 fusion.255
  229.2 5.3 copy.89
  234.5 6.7 copy.92
  241.2 4.8 copy.88
  246.0 6.6 copy.91
  252.7 97.3 %while.50 = (s32[]{:T(128)}, bf16[12,512,64]{1,2,0:T(8,128)(2,1)S(1)}, f32[12,512]{1,0:T(8,128)S(1)}, s32[1,1,512]{2,1,0:T(1,128)S(1)}, bf16[12,512,64]{2,1,0:T(...) while((s32[]{:T(128)}, ...), condition=%wide.region_5.6_spmd.clone, body=%wide.region_2.5_spmd.clone.sunk | while | flops 277872128 | bytes 30730372 | solution.py:72
  257.5 3.3 fusion.251
  265.6 3.3 fusion.251
  273.7 3.3 fusion.251
  281.8 3.3 fusion.251
  289.9 3.3 fusion.251
  298.0 3.3 fusion.251
  306.1 3.3 fusion.251
  322.3 3.3 fusion.251
  338.5 3.3 fusion.251
  356.2 7.3 fusion.171
  363.5 4.9 fusion.170
  368.4 9.7 convert_reduce_fusion.1
  378.2 6.2 fusion.182
  384.9 8.8 convert_reduce_fusion
  393.7 3.8 multiply_reduce_fusion.2
  407.7 130.5 %while.52 = (s32[]{:T(128)}, bf16[12,512,64]{1,2,0:T(8,128)(2,1)}, bf16[12,2048,64]{1,2,0:T(8,128)(2,1)S(1)}, bf16[12,2048,64]{1,2,0:T(8,128)(2,1)}, s32[1,1,512...) while((s32[]{:T(128)}, bf16[12,512,64]{1,2,0:T(8,128)(2,1)}, ...), condition=%wide.region_20.21_spmd.clone, body=%wide.region_18.20_spmd.clone.sunk | while | flops 681737728 | bytes 34655352 | solution.py:106
  538.3 4.3 convolution_convert_fusion
  548.4 139.2 %while.53 = (s32[]{:T(128)}, bf16[12,512,64]{1,2,0:T(8,128)(2,1)}, bf16[12,2048,64]{1,2,0:T(8,128)(2,1)S(1)}, bf16[12,2048,64]{1,2,0:T(8,128)(2,1)}, s32[1,1,512...) while((s32[]{:T(128)}, bf16[12,512,64]{1,2,0:T(8,128)(2,1)}, ...), condition=%wide.region_29.30_spmd.clone, body=%wide.region_27.29_spmd.clone.sunk | while | flops 681737728 | bytes 34655352 | solution.py:106
  693.4 6.3 fusion.150
  699.7 9.0 add_convert_fusion
  709.4 5.4 fusion.169
  714.8 4.8 add_convert_fusion.1
  721.0 6.9 fusion.135
  727.9 39.5 %reduce-scatter.15.cloned.1.call-done = bf16[512,768]{0,1:T(8,128)(2,1)} async-done(((bf16[2048,768]{0,1:T(8,128)(2,1)}), bf16[512,768]{0,1:T(8,128)(2,1)}) %reduce-scatter.15.cloned.1.call-update) | async-done | bytes 786448 | tf_op jit(solution)/shard_map/reduce_scatter | solution.py:181
  767.4 7.9 add_convert_fusion.2
  783.6 4.9 fusion.134
  788.6 4.4 fusion.121
  796.8 49.8 %reduce-scatter.23.cloned.1.call-done = bf16[768,768]{1,0:T(8,128)(2,1)} async-done(((bf16[3072,768]{1,0:T(8,128)(2,1)}), bf16[768,768]{1,0:T(8,128)(2,1)}) %reduce-scatter.23.cloned.1.call-update) | async-done | bytes 1179664 | tf_op jit(solution)/shard_map/reduce_scatter | solution.py:263
  846.6 50.4 %reduce-scatter.21.cloned.1.call-done = bf16[192,3072]{1,0:T(8,128)(2,1)} async-done(((bf16[768,3072]{1,0:T(8,128)(2,1)}), bf16[192,3072]{1,0:T(8,128)(2,1)}) %reduce-scatter.21.cloned.1.call-update) | async-done | bytes 1179664 | tf_op jit(solution)/shard_map/reduce_scatter | solution.py:257
  897.0 42.8 %reduce-scatter.17.cloned.1.call-done = bf16[192,2304]{1,0:T(8,128)(2,1)} async-done(((bf16[768,2304]{1,0:T(8,128)(2,1)}), bf16[192,2304]{1,0:T(8,128)(2,1)}) %reduce-scatter.17.cloned.1.call-update) | async-done | bytes 884752 | tf_op jit(solution)/shard_map/reduce_scatter | solution.py:239
  941.2 10.5 all-reduce.17
  952.5 23.8 %all-reduce.15 = (bf16[1536]{0:T(1024)(128)(2,1)S(1)}, bf16[192]{0:T(256)(128)(2,1)S(1)}, bf16[384]{0:T(512)(128)(2,1)S(1)}, bf16[192]{0:T(256)(128)(2,1)S(1)}, ...) all-reduce(bf16[1536]{0:T(1024)(128)(2,1)S(1)} %dynamic-update-slic, ...), channel_id=2, replica_groups=mesh['dp'=8,'band'=4] {'dp'}, use_global_device_ids=true, to_apply=%add.6 | all-reduce | flops 3648 | bytes 14592
  985.2 8.3 fusion.132
  993.6 8.4 fusion.133
  1003.3 80.3 %all-reduce.21.cloned.1.call-done = (bf16[192,2304]{1,0:T(8,128)(2,1)}, bf16[192,768]{1,0:T(8,128)(2,1)}, bf16[192,3072]{1,0:T(8,128)(2,1)}, bf16[768,768]{1,0:T(8,128)(2,1)}) async-done(((bf16[192,2304]{1,0:T(8,128)(2,1)}, bf16[192,768]{1,0:T(8,128)(2,1)}, bf16[192,3072]{1,0:T(8,128)(2,1)}, bf16[768,768]{1,0:T(8,128)(2,1)}), (bf16[192,2304]{1,0:T(8,128)(2,1)}, bf16[192,768]{1,0:T(8,128)(2,1)}, ...) | async-done | bytes 3538960 | tf_op jit(solution)/shard_map/psum | solution.py:275
  (740 shorter events, 483.4 us)
Async XLA Ops:
  7.2 28.2 %copy-start.2 = (bf16[2,1,512,768]{3,2,1,0:T(8,128)(2,1)S(1)}, bf16[2,1,512,768]{3,2,1,0:T(8,128)(2,1)}, u32[]{:S(2)}) copy-start(bf16[2,1,512,768]{3,2,1,0:T(8,128)(2,1)} %param.23) | copy-start | bytes 4718596
  7.2 36.0 %all-gather.12.cloned.1.call-start = ((), (), s32[]{:S(2)}) async-start(), calls=%async_computation.8 | async-start | bytes 4423680 | tf_op jit(solution)/shard_map/all_gather | solution.py:218
  7.9 73.6 %all-gather.26.cloned.1.call-start = ((), (), s32[]{:S(2)}) async-start(), calls=%async_computation.15 | async-start | bytes 3932160 | tf_op jit(solution)/shard_map/all_gather | solution.py:143
  27.6 19.9 %copy-start.37 = (f32[768]{0:T(1024)}, f32[768]{0:T(1024)S(1)}, u32[]{:S(2)}) copy-start(f32[768]{0:T(1024)S(1)} %convert_element_type.380) | copy-start | bytes 9220
  27.7 19.9 %copy-start.60 = (f32[768]{0:T(1024)}, f32[768]{0:T(1024)S(1)}, u32[]{:S(2)}) copy-start(f32[768]{0:T(1024)S(1)} %convert_element_type.381) | copy-start | bytes 9220
  35.4 12.2 %copy-start.40 = (f32[512]{0:T(512)}, f32[512]{0:T(512)S(1)}, u32[]{:S(2)}) copy-start(f32[512]{0:T(512)S(1)} %get-tuple-element.770) | copy-start | bytes 6148
  35.4 12.2 %copy-start.42 = (f32[512]{0:T(512)}, f32[512]{0:T(512)S(1)}, u32[]{:S(2)}) copy-start(f32[512]{0:T(512)S(1)} %get-tuple-element.771) | copy-start | bytes 6148
  36.6 11.0 %copy-start.46 = (f32[512]{0:T(512)}, f32[512]{0:T(512)S(1)}, u32[]{:S(2)}) copy-start(f32[512]{0:T(512)S(1)} %fusion.142) | copy-start | bytes 6148
  36.6 11.0 copy-start.44
  43.2 4.4 copy-start.72
  52.7 59.5 %all-gather.24.cloned.1.call-start = ((), (), s32[]{:S(2)}) async-start(), calls=%async_computation.14 | async-start | bytes 3932160 | tf_op jit(solution)/shard_map/all_gather | solution.py:142
  55.2 174.0 %all-gather.16.cloned.1.call-start = ((), (), s32[]{:S(2)}) async-start(), calls=%async_computation.10 | async-start | bytes 3932160 | tf_op jit(solution)/shard_map/all_gather | solution.py:143
  55.7 4.6 copy-start.64
  55.8 4.7 copy-start.69
  55.8 185.4 %all-gather.14.cloned.1.call-start = ((), (), s32[]{:S(2)}) async-start(), calls=%async_computation.9 | async-start | bytes 3932160 | tf_op jit(solution)/shard_map/all_gather | solution.py:142
  58.2 291.7 %all-gather.18.cloned.1.call-start = ((), (), s32[]{:S(2)}) async-start(), calls=%async_computation.11 | async-start | bytes 1474560 | tf_op jit(solution)/shard_map/all_gather | solution.py:220
  58.8 297.3 %all-gather.20.cloned.1.call-start = ((), (), s32[]{:S(2)}) async-start(), calls=%async_computation.12 | async-start | bytes 5898240 | tf_op jit(solution)/shard_map/all_gather | solution.py:224
  59.6 308.9 %all-gather.22.cloned.1.call-start = ((), (), s32[]{:S(2)}) async-start(), calls=%async_computation.13 | async-start | bytes 5898240 | tf_op jit(solution)/shard_map/all_gather | solution.py:226
  60.3 659.6 %reduce-scatter.11.cloned.1.call-start = ((), (), s32[]{:S(2)}) async-start(), calls=%async_computation.17 | async-start | bytes 3932160 | tf_op jit(solution)/shard_map/reduce_scatter | solution.py:181
  60.4 303.0 %copy-start.62 = (f32[768]{0:T(1024)}, f32[768]{0:T(1024)S(1)}, u32[]{:S(2)}) copy-start(f32[768]{0:T(1024)S(1)} %convert_element_type.391) | copy-start | bytes 9220
  229.1 5.3 copy-start.20
  229.1 5.3 copy-start.34
  229.1 5.3 copy-start.39
  353.4 44.1 %copy-start.13 = (f32[512,768]{1,0:T(8,128)}, f32[512,768]{1,0:T(8,128)S(1)}, u32[]{:S(2)}) copy-start(f32[512,768]{1,0:T(8,128)S(1)} %get-tuple-element.761) | copy-start | bytes 4718596
  356.2 7.3 copy-start.17
  356.2 7.3 copy-start.71
  363.5 5.0 copy-start.10
  378.1 6.2 copy-start.80
  378.1 6.2 copy-start.70
  378.2 6.8 copy-start.79
  378.2 15.6 %slice-start = ((s8[4718592]{0:T(1024)(128)(4,1)}), s8[4194304]{0:T(1024)(128)(4,1)S(1)}, s32[]{:S(2)}) async-start(s8[4718592]{0:T(1024)(128)(4,1)} %bitcast.464), calls=%async_computation.25 | async-start | bytes 8388608
  384.9 8.8 copy-start.18
  384.9 8.8 slice-start.1
  538.2 4.4 copy-start.9
  538.2 181.6 %reduce-scatter.9.cloned.1.call-start = ((), (), s32[]{:S(2)}) async-start(), calls=%async_computation.16 | async-start | bytes 3932160 | tf_op jit(solution)/shard_map/reduce_scatter | solution.py:178
  544.9 183.0 %reduce-scatter.13.cloned.1.call-start = ((), (), s32[]{:S(2)}) async-start(), calls=%async_computation.18 | async-start | bytes 3932160 | tf_op jit(solution)/shard_map/reduce_scatter | solution.py:178
  689.3 78.1 %reduce-scatter.15.cloned.1.call-start = ((), (), s32[]{:S(2)}) async-start(), calls=%async_computation.19 | async-start | bytes 3932160 | tf_op jit(solution)/shard_map/reduce_scatter | solution.py:181
  689.9 106.8 %reduce-scatter.19.cloned.1.call-start = ((), (), s32[]{:S(2)}) async-start(), calls=%async_computation.21 | async-start | bytes 1474560 | tf_op jit(solution)/shard_map/reduce_scatter | solution.py:245
  693.3 153.3 %reduce-scatter.23.cloned.1.call-start = ((), (), s32[]{:S(2)}) async-start(), calls=%async_computation.23 | async-start | bytes 5898240 | tf_op jit(solution)/shard_map/reduce_scatter | solution.py:263
  708.7 6.0 copy-start.14
  708.7 188.3 %reduce-scatter.21.cloned.1.call-start = ((), (), s32[]{:S(2)}) async-start(), calls=%async_computation.22 | async-start | bytes 5898240 | tf_op jit(solution)/shard_map/reduce_scatter | solution.py:257
  709.4 5.4 copy-start.82
  719.6 220.2 %reduce-scatter.17.cloned.1.call-start = ((), (), s32[]{:S(2)}) async-start(), calls=%async_computation.20 | async-start | bytes 4423680 | tf_op jit(solution)/shard_map/reduce_scatter | solution.py:239
  721.0 46.4 %copy-start.41 = (f32[512]{0:T(512)S(1)}, f32[512]{0:T(512)}, u32[]{:S(2)}) copy-start(f32[512]{0:T(512)} %copy-done.40) | copy-start | bytes 6148
  721.0 46.4 %copy-start.45 = (f32[512]{0:T(512)S(1)}, f32[512]{0:T(512)}, u32[]{:S(2)}) copy-start(f32[512]{0:T(512)} %copy-done.44) | copy-start | bytes 6148
  775.3 3.9 copy-start.77
  775.3 6.9 copy-start.67
  775.3 6.9 copy-start.68
  775.3 6.9 copy-start.65
  775.3 6.9 copy-start.66
  775.3 6.9 copy-start.56
  775.3 6.9 copy-start.57
  775.3 6.9 copy-start.58
  775.3 6.9 copy-start.59
  775.4 308.2 %all-reduce.21.cloned.1.call-start = ((), (), s32[]{:S(2)}) async-start(), calls=%async_computation.24 | async-start | bytes 7077888 | tf_op jit(solution)/shard_map/psum | solution.py:275
  783.6 4.9 copy-start.33
  783.6 4.9 copy-start.73
  783.6 4.9 copy-start.76
  788.6 4.5 copy-start.12
  788.6 4.4 copy-start.55
  788.6 4.4 copy-start.53
  796.7 184.3 %copy-start.5 = (f32[512,768]{1,0:T(8,128)S(1)}, f32[512,768]{1,0:T(8,128)}, u32[]{:S(2)}) copy-start(f32[512,768]{1,0:T(8,128)} %copy-done.4) | copy-start | bytes 4718596
  796.7 184.3 %copy-start.49 = (f32[512]{0:T(512)S(1)}, f32[512]{0:T(512)}, u32[]{:S(2)}) copy-start(f32[512]{0:T(512)} %copy-done.48) | copy-start | bytes 6148
  985.2 8.3 copy-start.15
  (60 other events, 115.3 us)
Sparse Core Ops, SparseCore 0:
  9.6 33.6 all-gather.11
  52.8 28.6 all-gather.25
  83.6 28.4 all-gather.23
  114.2 28.4 all-gather.15
  144.1 28.4 all-gather.13
  174.1 17.4 all-gather.17
  193.1 37.4 all-gather.19
  232.1 37.4 all-gather.21
  538.4 37.8 reduce-scatter.10
  578.6 37.7 reduce-scatter.8
  689.4 37.8 reduce-scatter.12
  729.7 37.7 reduce-scatter.14
  770.6 25.6 reduce-scatter.18
  798.6 47.9 reduce-scatter.22
  849.0 47.9 reduce-scatter.20
  899.4 40.3 reduce-scatter.16
  943.6 139.8 all-reduce.20
